TPU v7x, 128 devices: a whole 4x4x4 slice. The times are simulated.
128 devices in a mesh: dp: 32 (over z, x, core), seq: 4 (over y).
Axes of the slice: x: 4, y: 4, z: 4, core: 2. Of those that a mesh axis runs over, the one named last changes fastest.
Arguments:
- queries: bfloat16 [32768, 2560], P(('dp', 'seq')), may hold values from -200 to 200
- keys: bfloat16 [32768, 2560], P(('dp', 'seq')), may hold values from -200 to 200
- values: bfloat16 [32768, 2560], P(('dp', 'seq')), may hold values from -6 to 6
- gain_q: float32 [2560], replicated, may hold values from 0.5 to 1.5
- gain_k: float32 [2560], replicated, may hold values from 0.5 to 1.5
- tile_pairs: int32 [16, 8], replicated, may hold values from 0 to 15, as said below
- tile_lens: int32 [32, 16], P('dp'), may hold values from 40 to 64
- out_grad: bfloat16 [32768, 5120], P(('dp', 'seq')), may hold values from -24 to 24
- w_out: bfloat16 [5120, 2560], P('dp', 'seq'), may hold values from -0.125 to 0.125
Outputs:
- grad_q: bfloat16 [32768, 2560], P(('dp', 'seq'))
- grad_k: bfloat16 [32768, 2560], P(('dp', 'seq'))
- grad_v: bfloat16 [32768, 2560], P(('dp', 'seq'))
- grad_w: float32 [5120, 2560], P('dp', 'seq')
Inputs may be any that keep to these rules, and one draw needn't show every extreme that they name: `tile_pairs`: row a lists 8 different tiles of the window, with tile a first.
All inputs are finite; a program needn't handle non-finite values.
Results may differ from a plain program's by a relative error of at most 0.02.
Values may be sent and summed in bfloat16 or wider, within the bound.
No kernel may reach another device: no remote copies, remote signals or barrier semaphores. Data moves between devices by JAX's collectives and lax.ppermute only.
A program may use at most 128 MiB of HBM per device.

v0:
```python
import math
import jax
import jax.numpy as jnp
from jax import lax
from jax.sharding import PartitionSpec as P

HEAD_DIM = 128
EPS = 1e-06


def multiply(pattern, left, right):
    return jnp.einsum(pattern, left, right, preferred_element_type=jnp.float32)


def normalize(field, gain):
    values_f = field.astype(jnp.float32)
    row_scale = lax.rsqrt(jnp.mean(values_f * values_f, axis=-1, keepdims=True) + EPS)
    return ((values_f * row_scale * gain).astype(jnp.bfloat16), row_scale)


def norm_finish(values_f, row_scale, gated, inner, width):
    return (row_scale * gated - values_f * row_scale**3 * inner / width).astype(jnp.bfloat16)


def tile_attention(query_tiles, key_tiles, value_tiles, grad_tiles, tile_pairs, live_lengths):
    tile_count, tile_rows, head_width = query_tiles.shape
    neighbours = tile_pairs.shape[1]
    factor = 1.0 / math.sqrt(head_width)
    key_near = jnp.take(key_tiles, tile_pairs, axis=0).reshape(
        tile_count, neighbours * tile_rows, head_width
    )
    value_near = jnp.take(value_tiles, tile_pairs, axis=0).reshape(
        tile_count, neighbours * tile_rows, head_width
    )
    near_lengths = jnp.take(live_lengths, tile_pairs, axis=0)
    live = (
        jnp.arange(tile_rows, dtype=jnp.int32)[None, None, :] < near_lengths[:, :, None]
    ).reshape(tile_count, neighbours * tile_rows)
    scores = multiply("aqd,akd->aqk", query_tiles, key_near) * factor
    scores = jnp.where(live[:, None, :], scores, -jnp.inf)
    row_max = jnp.max(scores, axis=-1, keepdims=True)
    weights = jnp.exp(scores - row_max)
    probs = weights / jnp.sum(weights, axis=-1, keepdims=True)
    probs_low = probs.astype(jnp.bfloat16)
    attended = multiply("aqk,akd->aqd", probs_low, value_near).astype(jnp.bfloat16)
    grad_probs = multiply("aqd,akd->aqk", grad_tiles, value_near)
    delta = jnp.sum(probs * grad_probs, axis=-1, keepdims=True)
    grad_scores = (probs * (grad_probs - delta)).astype(jnp.bfloat16)
    grad_query = (multiply("aqk,akd->aqd", grad_scores, key_near) * factor).astype(jnp.bfloat16)
    grad_key_near = multiply("aqk,aqd->akd", grad_scores, query_tiles) * factor
    grad_value_near = multiply("aqk,aqd->akd", probs_low, grad_tiles)
    owners = (
        tile_pairs[:, :, None] == jnp.arange(tile_count, dtype=jnp.int32)[None, None, :]
    ).astype(jnp.float32)
    grad_key = jnp.einsum(
        "anb,antd->btd",
        owners,
        grad_key_near.reshape(tile_count, neighbours, tile_rows, head_width),
        precision=lax.Precision.HIGHEST,
    ).astype(jnp.bfloat16)
    grad_value = jnp.einsum(
        "anb,antd->btd",
        owners,
        grad_value_near.reshape(tile_count, neighbours, tile_rows, head_width),
        precision=lax.Precision.HIGHEST,
    ).astype(jnp.bfloat16)
    return (attended, grad_query, grad_key, grad_value)


def per_device(queries, keys, values, gain_q, gain_k, tile_pairs, tile_lens, out_grad, w_out):
    seq_count = lax.axis_size("seq")
    dp_count = lax.axis_size("dp")
    tok_rows = queries.shape[0]
    width = queries.shape[1]
    local_width = width // seq_count
    clip_rows = tok_rows * seq_count
    tile_count = tile_pairs.shape[0]
    tile_rows = clip_rows // tile_count
    head_count = local_width // HEAD_DIM
    clip_lengths = tile_lens[0]
    query_normed, query_scale = normalize(queries, gain_q)
    key_normed, key_scale = normalize(keys, gain_k)
    query_heads, key_heads, value_heads = (
        lax.all_to_all(query_normed, "seq", split_axis=1, concat_axis=0, tiled=True),
        lax.all_to_all(key_normed, "seq", split_axis=1, concat_axis=0, tiled=True),
        lax.all_to_all(values, "seq", split_axis=1, concat_axis=0, tiled=True),
    )
    cot_all = lax.all_gather(out_grad, "seq", axis=0, tiled=True)
    columns = cot_all
    grad_attended = jnp.dot(
        columns, lax.all_gather(w_out, "dp", axis=0, tiled=True), preferred_element_type=jnp.float32
    ).astype(jnp.bfloat16)

    def split(field):
        return field.reshape(tile_count, tile_rows, head_count, HEAD_DIM).transpose(2, 0, 1, 3)

    def merge(field):
        return field.transpose(1, 2, 0, 3).reshape(clip_rows, local_width)

    def one_head(group):
        return tile_attention(group[0], group[1], group[2], group[3], tile_pairs, clip_lengths)

    attended, grad_qn, grad_kn, grad_vh = lax.map(
        one_head, (split(query_heads), split(key_heads), split(value_heads), split(grad_attended))
    )
    attended = merge(attended)
    grad_qn = merge(grad_qn)
    grad_kn = merge(grad_kn)
    grad_vh = merge(grad_vh)
    columns = cot_all
    grad_w = lax.psum_scatter(
        (
            jnp.einsum("td,te->de", columns, attended, preferred_element_type=jnp.float32)
            / dp_count
        ).astype(jnp.bfloat16),
        "dp",
        scatter_dimension=0,
        tiled=True,
    ).astype(jnp.float32)
    grad_qt, grad_kt, grad_v = (
        lax.all_to_all(grad_qn, "seq", split_axis=0, concat_axis=1, tiled=True),
        lax.all_to_all(grad_kn, "seq", split_axis=0, concat_axis=1, tiled=True),
        lax.all_to_all(grad_vh, "seq", split_axis=0, concat_axis=1, tiled=True),
    )
    query_full = queries.astype(jnp.float32)
    key_full = keys.astype(jnp.float32)
    gated_q = gain_q * grad_qt.astype(jnp.float32)
    gated_k = gain_k * grad_kt.astype(jnp.float32)
    inner_q = jnp.sum(gated_q * query_full, axis=-1, keepdims=True)
    inner_k = jnp.sum(gated_k * key_full, axis=-1, keepdims=True)
    grad_q = norm_finish(query_full, query_scale, gated_q, inner_q, width)
    grad_k = norm_finish(key_full, key_scale, gated_k, inner_k, width)
    return (grad_q, grad_k, grad_v, grad_w)


def solution(mesh):
    return jax.shard_map(
        per_device,
        mesh=mesh,
        in_specs=(
            P(("dp", "seq"), None),
            P(("dp", "seq"), None),
            P(("dp", "seq"), None),
            P(),
            P(),
            P(),
            P("dp", None),
            P(("dp", "seq"), None),
            P("dp", "seq"),
        ),
        out_specs=(
            P(("dp", "seq"), None),
            P(("dp", "seq"), None),
            P(("dp", "seq"), None),
            P("dp", "seq"),
        ),
        check_vma=False,
    )
```

profile of v0, /device:TPU:0, one launch (start us, length us, event | category | flops | bytes accessed | tf_op | source)
XLA Modules:
  0.0 484.7 jit_solution(18076181013758219229)
XLA Ops:
  12.3 4.5 all-to-all-start
  23.3 11.4 %all-to-all-done = bf16[256,4,640]{2,0,1:T(8,128)(2,1)S(1)} async-done(((bf16[256,4,640]{2,0,1:T(8,128)(2,1)}), bf16[256,4,640]{2,0,1:T(8,128)(2,1)S(1)}, u32[]{:S(2)}, u32[]{:S(2)}) %all-to-all-start) | async-done | bytes 1310752 | tf_op jit(solution)/shard_map/all_to_all | solution.py:84
  40.8 14.4 %all-to-all-done.1 = bf16[256,4,640]{2,0,1:T(8,128)(2,1)S(1)} async-done(((bf16[256,4,640]{2,0,1:T(8,128)(2,1)}), bf16[256,4,640]{2,0,1:T(8,128)(2,1)S(1)}, u32[]{:S(2)}, u32[]{:S(2)}) %all-to-all-start.1) | async-done | bytes 1310752 | tf_op jit(solution)/shard_map/all_to_all | solution.py:85
  55.2 4.3 all-to-all-start.2
  67.6 8.1 %all-to-all-done.2 = bf16[256,4,640]{2,0,1:T(8,128)(2,1)} async-done(((bf16[256,4,640]{2,0,1:T(8,128)(2,1)}), bf16[256,4,640]{2,0,1:T(8,128)(2,1)}, u32[]{:S(2)}, u32[]{:S(2)}) %all-to-all-start.2) | async-done | bytes 1310752 | tf_op jit(solution)/shard_map/all_to_all | solution.py:86
  80.3 83.5 %all-gather.3.cloned.1.call-done = bf16[1024,5120]{1,0:T(8,128)(2,1)} async-done(((bf16[256,5120]{1,0:T(8,128)(2,1)}), bf16[1024,5120]{1,0:T(8,128)(2,1)}) %all-gather.3.cloned.1.call-update) | async-done | bytes 10485776 | tf_op jit(solution)/shard_map/all_gather | solution.py:88
  163.8 13.7 %convolution_convert_fusion.1 = bf16[1024,640]{1,0:T(8,128)(2,1)} fusion(bf16[1024,5120]{1,0:T(8,128)(2,1)} %all-gather.3.cloned.1.call-done, bf16[5120,640]{1,0:T(8,128)(2,1)} %all-gather.5.cloned.1.call-done), kind=kOutput, calls=%fused_computation.95 | convolution fusion | flops 6711541760 | bytes 18350080 | tf_op jit(solution)/shard_map/dot_general | solution.py:90
  182.1 182.6 %while.18 = (s32[]{:T(128)}, bf16[5,16,64,128]{3,2,1,0:T(8,128)(2,1)}, bf16[5,16,64,128]{3,2,1,0:T(8,128)(2,1)}, bf16[5,16,64,128]{3,1,2,0:T(8,128)(2,1)}, bf16[...) while((s32[]{:T(128)}, ...), condition=%wide.region_6.8_spmd, body=%wide.region_2.7_spmd.sunk | while | flops 1219638656 | bytes 88276472 | solution.py:103
  187.9 4.0 broadcast_select_fusion.6
  204.6 7.3 %fusion.138 = bf16[5,16,64,128]{3,1,2,0:T(8,128)(2,1)} fusion(bf16[5,16,64,128]{3,1,2,0:T(8,128)(2,1)} %get-tuple-element.341, s32[]{:T(128)S(6)} %copy.142, f32[16,8,64,128]{3,2,1,0:T(8,128)} %bitcast.172, s32[16,8]{0,1:T(8,128)S(1)} %copy.132), kind=kOutput, calls=%fused_computation.26.clone.1 | convolution fusion | flops 201459712 | bytes 4456964 | tf_op jit(solution)/shard_map/while/body/eval_jaxpr/anb,antd->btd/dot_general | solution.py:55
  213.8 5.1 %fusion.140 = bf16[5,16,64,128]{3,1,2,0:T(8,128)(2,1)} fusion(bf16[5,16,64,128]{3,1,2,0:T(8,128)(2,1)} %get-tuple-element.342, s32[]{:T(128)S(6)} %copy.142, f32[16,8,64,128]{3,2,1,0:T(8,128)S(1)} %bitcast.177, s32[16,8]{0,1:T(8,128)S(1)} %copy.132), kind=kOutput, calls=%fused_computation.28.clone.1 | convolution fusion | flops 201459712 | bytes 4456964 | tf_op jit(solution)/shard_map/while/body/eval_jaxpr/anb,antd->btd/dot_general | solution.py:61
  224.3 4.0 broadcast_select_fusion.6
  230.9 3.6 fusion.136
  240.9 7.3 %fusion.138 = bf16[5,16,64,128]{3,1,2,0:T(8,128)(2,1)} fusion(bf16[5,16,64,128]{3,1,2,0:T(8,128)(2,1)} %get-tuple-element.341, s32[]{:T(128)S(6)} %copy.142, f32[16,8,64,128]{3,2,1,0:T(8,128)} %bitcast.172, s32[16,8]{0,1:T(8,128)S(1)} %copy.132), kind=kOutput, calls=%fused_computation.26.clone.1 | convolution fusion | flops 201459712 | bytes 4456964 | tf_op jit(solution)/shard_map/while/body/eval_jaxpr/anb,antd->btd/dot_general | solution.py:55
  250.1 5.1 %fusion.140 = bf16[5,16,64,128]{3,1,2,0:T(8,128)(2,1)} fusion(bf16[5,16,64,128]{3,1,2,0:T(8,128)(2,1)} %get-tuple-element.342, s32[]{:T(128)S(6)} %copy.142, f32[16,8,64,128]{3,2,1,0:T(8,128)S(1)} %bitcast.177, s32[16,8]{0,1:T(8,128)S(1)} %copy.132), kind=kOutput, calls=%fused_computation.28.clone.1 | convolution fusion | flops 201459712 | bytes 4456964 | tf_op jit(solution)/shard_map/while/body/eval_jaxpr/anb,antd->btd/dot_general | solution.py:61
  260.7 4.0 broadcast_select_fusion.6
  277.3 7.2 %fusion.138 = bf16[5,16,64,128]{3,1,2,0:T(8,128)(2,1)} fusion(bf16[5,16,64,128]{3,1,2,0:T(8,128)(2,1)} %get-tuple-element.341, s32[]{:T(128)S(6)} %copy.142, f32[16,8,64,128]{3,2,1,0:T(8,128)} %bitcast.172, s32[16,8]{0,1:T(8,128)S(1)} %copy.132), kind=kOutput, calls=%fused_computation.26.clone.1 | convolution fusion | flops 201459712 | bytes 4456964 | tf_op jit(solution)/shard_map/while/body/eval_jaxpr/anb,antd->btd/dot_general | solution.py:55
  286.5 5.1 %fusion.140 = bf16[5,16,64,128]{3,1,2,0:T(8,128)(2,1)} fusion(bf16[5,16,64,128]{3,1,2,0:T(8,128)(2,1)} %get-tuple-element.342, s32[]{:T(128)S(6)} %copy.142, f32[16,8,64,128]{3,2,1,0:T(8,128)S(1)} %bitcast.177, s32[16,8]{0,1:T(8,128)S(1)} %copy.132), kind=kOutput, calls=%fused_computation.28.clone.1 | convolution fusion | flops 201459712 | bytes 4456964 | tf_op jit(solution)/shard_map/while/body/eval_jaxpr/anb,antd->btd/dot_general | solution.py:61
  297.1 4.0 broadcast_select_fusion.6
  313.7 7.3 %fusion.138 = bf16[5,16,64,128]{3,1,2,0:T(8,128)(2,1)} fusion(bf16[5,16,64,128]{3,1,2,0:T(8,128)(2,1)} %get-tuple-element.341, s32[]{:T(128)S(6)} %copy.142, f32[16,8,64,128]{3,2,1,0:T(8,128)} %bitcast.172, s32[16,8]{0,1:T(8,128)S(1)} %copy.132), kind=kOutput, calls=%fused_computation.26.clone.1 | convolution fusion | flops 201459712 | bytes 4456964 | tf_op jit(solution)/shard_map/while/body/eval_jaxpr/anb,antd->btd/dot_general | solution.py:55
  322.9 5.2 %fusion.140 = bf16[5,16,64,128]{3,1,2,0:T(8,128)(2,1)} fusion(bf16[5,16,64,128]{3,1,2,0:T(8,128)(2,1)} %get-tuple-element.342, s32[]{:T(128)S(6)} %copy.142, f32[16,8,64,128]{3,2,1,0:T(8,128)S(1)} %bitcast.177, s32[16,8]{0,1:T(8,128)S(1)} %copy.132), kind=kOutput, calls=%fused_computation.28.clone.1 | convolution fusion | flops 201459712 | bytes 4456964 | tf_op jit(solution)/shard_map/while/body/eval_jaxpr/anb,antd->btd/dot_general | solution.py:61
  333.5 4.0 broadcast_select_fusion.6
  340.1 3.6 fusion.136
  350.1 7.3 %fusion.138 = bf16[5,16,64,128]{3,1,2,0:T(8,128)(2,1)} fusion(bf16[5,16,64,128]{3,1,2,0:T(8,128)(2,1)} %get-tuple-element.341, s32[]{:T(128)S(6)} %copy.142, f32[16,8,64,128]{3,2,1,0:T(8,128)} %bitcast.172, s32[16,8]{0,1:T(8,128)S(1)} %copy.132), kind=kOutput, calls=%fused_computation.26.clone.1 | convolution fusion | flops 201459712 | bytes 4456964 | tf_op jit(solution)/shard_map/while/body/eval_jaxpr/anb,antd->btd/dot_general | solution.py:55
  359.3 5.2 %fusion.140 = bf16[5,16,64,128]{3,1,2,0:T(8,128)(2,1)} fusion(bf16[5,16,64,128]{3,1,2,0:T(8,128)(2,1)} %get-tuple-element.342, s32[]{:T(128)S(6)} %copy.142, f32[16,8,64,128]{3,2,1,0:T(8,128)S(1)} %bitcast.177, s32[16,8]{0,1:T(8,128)S(1)} %copy.132), kind=kOutput, calls=%fused_computation.28.clone.1 | convolution fusion | flops 201459712 | bytes 4456964 | tf_op jit(solution)/shard_map/while/body/eval_jaxpr/anb,antd->btd/dot_general | solution.py:61
  367.0 11.5 %fusion.68 = bf16[5120,640]{0,1:T(8,128)(2,1)} fusion(bf16[1024,5120]{1,0:T(8,128)(2,1)} %all-gather.3.cloned.1.call-done, bf16[128,8,5,128]{3,2,1,0:T(8,128)(2,1)S(1)} %bitcast.191), kind=kOutput, calls=%fused_computation.66 | convolution fusion | flops 6717440000 | bytes 18350080 | tf_op jit(solution)/shard_map/td,te->de/dot_general | solution.py:113
  378.5 9.5 %copy.97 = bf16[5120,640]{1,0:T(8,128)(2,1)} copy(bf16[5120,640]{0,1:T(8,128)(2,1)} %fusion.68) | data formatting | bytes 13107200
  392.8 4.0 all-to-all-start.3
  406.2 8.4 %all-to-all-done.3 = bf16[4,256,640]{2,1,0:T(8,128)(2,1)S(1)} async-done(((bf16[4,256,640]{2,1,0:T(8,128)(2,1)}), bf16[4,256,640]{2,1,0:T(8,128)(2,1)S(1)}, u32[]{:S(2)}, u32[]{:S(2)}) %all-to-all-start.3) | async-done | bytes 1310752 | tf_op jit(solution)/shard_map/all_to_all | solution.py:121
  415.7 3.8 all-to-all-start.4
  432.7 3.7 all-to-all-done.4
  459.3 16.6 %reduce-scatter.4.cloned.1.call-done = bf16[160,640]{1,0:T(8,128)(2,1)} async-done(((bf16[5120,640]{1,0:T(8,128)(2,1)}), bf16[160,640]{1,0:T(8,128)(2,1)}) %reduce-scatter.4.cloned.1.call-update) | async-done | bytes 204816
  (232 shorter events, 182.6 us)
Async XLA Ops:
  7.2 52.7 %copy-start = (s32[1,16]{1,0:T(1,128)S(1)}, s32[1,16]{1,0:T(1,128)}, u32[]{:S(2)}) copy-start(s32[1,16]{1,0:T(1,128)} %param.19) | copy-start | bytes 196
  7.2 73.1 %all-gather.5.cloned.1.call-start = ((), (), s32[]{:S(2)}) async-start(), calls=%async_computation.8 | async-start | bytes 6758400 | tf_op jit(solution)/shard_map/all_gather | solution.py:91
  7.9 155.8 %all-gather.3.cloned.1.call-start = ((), (), s32[]{:S(2)}) async-start(), calls=%async_computation.7 | async-start | bytes 13107200 | tf_op jit(solution)/shard_map/all_gather | solution.py:88
  12.3 22.5 %all-to-all-start = ((bf16[256,4,640]{2,0,1:T(8,128)(2,1)}), bf16[256,4,640]{2,0,1:T(8,128)(2,1)S(1)}, u32[]{:S(2)}, u32[]{:S(2)}) async-start(bf16[256,4,640]{2,0,1:T(8,128)(2,1)} %copy.73), calls=%async_computation | async-start | bytes 2621440 | tf_op jit(solution)/shard_map/all_to_all | solution.py:84
  18.4 4.9 %copy-start.5 = (bf16[256,2560]{0,1:T(8,128)(2,1)}, bf16[256,2560]{0,1:T(8,128)(2,1)S(1)}, u32[]{:S(2)}) copy-start(bf16[256,2560]{0,1:T(8,128)(2,1)S(1)} %copy.74) | copy-start | bytes 3932164
  19.4 3.9 copy-start.21
  34.7 20.5 %all-to-all-start.1 = ((bf16[256,4,640]{2,0,1:T(8,128)(2,1)}), bf16[256,4,640]{2,0,1:T(8,128)(2,1)S(1)}, u32[]{:S(2)}, u32[]{:S(2)}) async-start(bf16[256,4,640]{2,0,1:T(8,128)(2,1)} %copy.75), calls=%async_computation.1 | async-start | bytes 2621440 | tf_op jit(solution)/shard_map/all_to_all | solution.py:85
  38.3 21.4 %copy-start.20 = (s32[16,8]{0,1:T(8,128)S(1)}, s32[16,8]{0,1:T(8,128)}, u32[]{:S(2)}) copy-start(s32[16,8]{0,1:T(8,128)} %param.18) | copy-start | bytes 1540
  55.2 5.9 %copy-start.11 = (bf16[256,4,640]{2,0,1:T(8,128)(2,1)}, bf16[256,4,640]{2,0,1:T(8,128)(2,1)S(1)}, u32[]{:S(2)}) copy-start(bf16[256,4,640]{2,0,1:T(8,128)(2,1)S(1)} %all-to-all-done.1) | copy-start | bytes 3932164
  55.2 20.5 %all-to-all-start.2 = ((bf16[256,4,640]{2,0,1:T(8,128)(2,1)}), bf16[256,4,640]{2,0,1:T(8,128)(2,1)}, u32[]{:S(2)}, u32[]{:S(2)}) async-start(bf16[256,4,640]{2,0,1:T(8,128)(2,1)} %bitcast.186), calls=%async_computation.2 | async-start | bytes 2621440 | tf_op jit(solution)/shard_map/all_to_all | solution.py:86
  59.6 416.4 %reduce-scatter.4.cloned.1.call-start = ((), (), s32[]{:S(2)}) async-start(), calls=%async_computation.9 | async-start | bytes 6758400
  194.5 3.6 copy-start.2
  194.5 3.6 copy-start.3
  204.6 7.3 %copy-start.4 = (f32[16,64,512]{2,1,0:T(8,128)S(1)}, f32[16,64,512]{2,1,0:T(8,128)}, u32[]{:S(2)}) copy-start(f32[16,64,512]{2,1,0:T(8,128)} %get-tuple-element.322) | copy-start | bytes 6291460 | tf_op jit(solution)/shard_map/while
  230.9 3.6 copy-start.2
  230.9 3.6 copy-start.3
  240.9 7.3 %copy-start.4 = (f32[16,64,512]{2,1,0:T(8,128)S(1)}, f32[16,64,512]{2,1,0:T(8,128)}, u32[]{:S(2)}) copy-start(f32[16,64,512]{2,1,0:T(8,128)} %get-tuple-element.322) | copy-start | bytes 6291460 | tf_op jit(solution)/shard_map/while
  267.3 3.6 copy-start.2
  267.3 3.6 copy-start.3
  277.3 7.3 %copy-start.4 = (f32[16,64,512]{2,1,0:T(8,128)S(1)}, f32[16,64,512]{2,1,0:T(8,128)}, u32[]{:S(2)}) copy-start(f32[16,64,512]{2,1,0:T(8,128)} %get-tuple-element.322) | copy-start | bytes 6291460 | tf_op jit(solution)/shard_map/while
  303.6 3.6 copy-start.2
  303.6 3.6 copy-start.3
  313.7 7.3 %copy-start.4 = (f32[16,64,512]{2,1,0:T(8,128)S(1)}, f32[16,64,512]{2,1,0:T(8,128)}, u32[]{:S(2)}) copy-start(f32[16,64,512]{2,1,0:T(8,128)} %get-tuple-element.322) | copy-start | bytes 6291460 | tf_op jit(solution)/shard_map/while
  340.1 3.6 copy-start.2
  340.1 3.6 copy-start.3
  350.1 7.3 %copy-start.4 = (f32[16,64,512]{2,1,0:T(8,128)S(1)}, f32[16,64,512]{2,1,0:T(8,128)}, u32[]{:S(2)}) copy-start(f32[16,64,512]{2,1,0:T(8,128)} %get-tuple-element.322) | copy-start | bytes 6291460 | tf_op jit(solution)/shard_map/while
  392.8 21.9 %all-to-all-start.3 = ((bf16[4,256,640]{2,1,0:T(8,128)(2,1)}), bf16[4,256,640]{2,1,0:T(8,128)(2,1)S(1)}, u32[]{:S(2)}, u32[]{:S(2)}) async-start(bf16[4,256,640]{2,1,0:T(8,128)(2,1)} %all_to_all.79), calls=%async_computation.3 | async-start | bytes 2621440 | tf_op jit(solution)/shard_map/all_to_all | solution.py:121
  415.7 20.7 %all-to-all-start.4 = ((bf16[4,256,640]{2,1,0:T(8,128)(2,1)}), bf16[4,256,640]{2,1,0:T(8,128)(2,1)S(1)}, u32[]{:S(2)}, u32[]{:S(2)}) async-start(bf16[4,256,640]{2,1,0:T(8,128)(2,1)} %all_to_all.81), calls=%async_computation.4 | async-start | bytes 2621440 | tf_op jit(solution)/shard_map/all_to_all | solution.py:122
  437.5 19.6 %all-to-all-start.5 = ((bf16[4,256,640]{2,1,0:T(8,128)(2,1)}), bf16[4,256,640]{2,1,0:T(8,128)(2,1)S(1)}, u32[]{:S(2)}, u32[]{:S(2)}) async-start(bf16[4,256,640]{2,1,0:T(8,128)(2,1)} %all_to_all.83), calls=%async_computation.5 | async-start | bytes 2621440 | tf_op jit(solution)/shard_map/all_to_all | solution.py:123
  444.0 3.4 copy-start.6
  444.0 3.4 copy-start.19
  457.1 20.8 %copy-start.1 = (s32[1,16]{1,0:T(1,128)S(1)}, s32[1,16]{1,0:T(1,128)}, u32[]{:S(2)}) copy-start(s32[1,16]{1,0:T(1,128)} %param.19) | copy-start | bytes 196
  (16 other events, 34.8 us)
Sparse Core Ops, SparseCore 0:
  10.3 52.1 all-gather.4
  64.1 99.5 all-gather.2
  388.1 87.7 reduce-scatter.3
where the time goes:
time: 494 us; the launch traced here: 485 us
  matrix products  156 us (32%)
  waiting for transfers between devices  151 us (31%)
  local copies, waits for them, and re-layouts  98.8 us (20%)
  other arithmetic  40.3 us (8%)
  starting transfers between devices  23.8 us (5%)
  between operations  14.3 us (3%)
    all_gather x1, waiting for transfers between devices, per_device(): cot_all = lax.all_gather(out_grad, 'seq', axis=0, tiled=True)  83.5 us
    dot_general x25, matrix products, multiply(): return jnp.einsum(pattern, left, right, preferred_element_type=jnp.float32)  57.5 us
    dot_general x5, matrix products, tile_attention(): jnp.einsum('anb,antd->btd', owners, grad_key_near.reshape(tile_count, nei...  36.3 us
    dot_general x5, matrix products, tile_attention(): jnp.einsum('anb,antd->btd', owners, grad_value_near.reshape(tile_count, n...  25.7 us
    unnamed x56, local copies, waits for them, and re-layouts  24 us
    select_n x5, other arithmetic, tile_attention(): jnp.take(key_tiles, tile_pairs, axis=0)  20.2 us
    unnamed x4, waiting for transfers between devices  18 us
    all_to_all x1, waiting for transfers between devices, per_device(): lax.all_to_all(key_normed, 'seq', split_axis=1, concat_axis=0, tiled=True)  14.4 us
  transfers between devices with their start and end apart: 9, of which 8 were waited for; matrix products, arithmetic and copies ran while one was open for 12% of the time, Pallas kernels for 0%

commit v1 on v0

--- a/solution.py
+++ b/solution.py
@@ -85,7 +85,10 @@
         lax.all_to_all(key_normed, "seq", split_axis=1, concat_axis=0, tiled=True),
         lax.all_to_all(values, "seq", split_axis=1, concat_axis=0, tiled=True),
     )
-    cot_all = lax.all_gather(out_grad, "seq", axis=0, tiled=True)
+    peers = lax.axis_size("seq")
+    tiles = jnp.stack([out_grad for _ in range(peers)])
+    tiles = lax.all_to_all(tiles, "seq", split_axis=0, concat_axis=0)
+    cot_all = jnp.concatenate(tiles, axis=0)
     columns = cot_all
     grad_attended = jnp.dot(
         columns, lax.all_gather(w_out, "dp", axis=0, tiled=True), preferred_element_type=jnp.float32

time: 494 us -> 533 us (1.079)
  blocking collectives: 0 us -> 20.4 us
  local copies, waits for them, and re-layouts: 98.8 us -> 107 us
  waiting for transfers between devices: 151 us -> 157 us
    all_to_all x1, waiting for transfers between devices: 8.08 us -> 101 us  [per_device(): tiles = lax.all_to_all(tiles, 'seq', split_axis=0, concat_axis=0)]
    all_gather x1 -> x0, waiting for transfers between devices: 83.5 us -> none  [per_device(): cot_all = lax.all_gather(out_grad, 'seq', axis=0, tiled=True)]
    all_to_all x0 -> x1, blocking collectives: none -> 20.4 us  [per_device(): lax.all_to_all(values, 'seq', split_axis=1, concat_axis=0, tiled=True)]
    unnamed x4 -> x3, waiting for transfers between devices: 18 us -> 26.5 us
    another operation x5 -> x6, local copies, waits for them, and re-layouts: 0.34 us -> 7.24 us  [the longest x1 6.9 us: per_device(): tiles = jnp.stack([out_grad for _ in range(peers)])]
    unnamed x56 -> x54, local copies, waits for them, and re-layouts: 24 us -> 25.2 us
  transfers between devices with their start and end apart: 9 -> 8, of which waited for: 8 -> 5; matrix products, arithmetic and copies ran while one was open for 12% -> 13% of each run, Pallas kernels for 0% -> 0%
where the time goes in v1:
time: 533 us; the launch traced here: 523 us
  waiting for transfers between devices  157 us (29%)
  matrix products  156 us (29%)
  local copies, waits for them, and re-layouts  107 us (20%)
  other arithmetic  40.3 us (8%)
  starting transfers between devices  26.4 us (5%)
  blocking collectives  20.4 us (4%)
  between operations  14.8 us (3%)
    all_to_all x1, waiting for transfers between devices, per_device(): tiles = lax.all_to_all(tiles, 'seq', split_axis=0, concat_axis=0)  101 us
    dot_general x25, matrix products, multiply(): return jnp.einsum(pattern, left, right, preferred_element_type=jnp.float32)  57.6 us
    dot_general x5, matrix products, tile_attention(): jnp.einsum('anb,antd->btd', owners, grad_key_near.reshape(tile_count, nei...  36.3 us
    unnamed x3, waiting for transfers between devices  26.5 us
    dot_general x5, matrix products, tile_attention(): jnp.einsum('anb,antd->btd', owners, grad_value_near.reshape(tile_count, n...  25.7 us
    unnamed x54, local copies, waits for them, and re-layouts  25.2 us
    all_to_all x1, blocking collectives, per_device(): lax.all_to_all(values, 'seq', split_axis=1, concat_axis=0, tiled=True)  20.4 us
    select_n x5, other arithmetic, tile_attention(): jnp.take(key_tiles, tile_pairs, axis=0)  20.1 us
  transfers between devices with their start and end apart: 8, of which 5 were waited for; matrix products, arithmetic and copies ran while one was open for 13% of the time, Pallas kernels for 0%

profile of v1, /device:TPU:0, one launch (start us, length us, event | category | flops | bytes accessed | tf_op | source)
XLA Modules:
  0.0 522.8 jit_solution(1043384552491140459)
XLA Ops:
  12.5 4.5 all-to-all-start
  23.6 11.4 %all-to-all-done = bf16[256,4,640]{2,0,1:T(8,128)(2,1)S(1)} async-done(((bf16[256,4,640]{2,0,1:T(8,128)(2,1)}), bf16[256,4,640]{2,0,1:T(8,128)(2,1)S(1)}, u32[]{:S(2)}, u32[]{:S(2)}) %all-to-all-start) | async-done | bytes 1310752 | tf_op jit(solution)/shard_map/all_to_all | solution.py:84
  41.0 14.5 %all-to-all-done.1 = bf16[256,4,640]{2,0,1:T(8,128)(2,1)S(1)} async-done(((bf16[256,4,640]{2,0,1:T(8,128)(2,1)}), bf16[256,4,640]{2,0,1:T(8,128)(2,1)S(1)}, u32[]{:S(2)}, u32[]{:S(2)}) %all-to-all-start.1) | async-done | bytes 1310752 | tf_op jit(solution)/shard_map/all_to_all | solution.py:85
  55.5 20.4 %all_to_all.98 = bf16[256,4,640]{2,0,1:T(8,128)(2,1)} all-to-all(bf16[256,4,640]{2,0,1:T(8,128)(2,1)} %bitcast.189), channel_id=1, replica_groups=mesh['dp'=32,'seq'=4] {'seq'}, dimensions={1} | all-to-all | bytes 2621440 | tf_op jit(solution)/shard_map/all_to_all | solution.py:86
  75.9 6.9 %stack.2 = bf16[4,256,5120]{2,1,0:T(8,128)(2,1)} broadcast(bf16[256,5120]{1,0:T(8,128)(2,1)} %param.20), dimensions={1,2} | broadcast | bytes 13107200 | tf_op jit(solution)/shard_map/stack | solution.py:89
  82.8 6.1 %all-to-all-start.3 = ((bf16[4,256,5120]{2,1,0:T(8,128)(2,1)}), bf16[4,256,5120]{2,1,0:T(8,128)(2,1)}, u32[]{:S(2)}, u32[]{:S(2)}) async-start(bf16[4,256,5120]{2,1,0:T(8,128)(2,1)} %stack.2), calls=%async_computation.3 | async-start | bytes 20971520 | tf_op jit(solution)/shard_map/all_to_all | solution.py:90
  101.5 100.6 %all-to-all-done.3 = bf16[4,256,5120]{2,1,0:T(8,128)(2,1)} async-done(((bf16[4,256,5120]{2,1,0:T(8,128)(2,1)}), bf16[4,256,5120]{2,1,0:T(8,128)(2,1)}, u32[]{:S(2)}, u32[]{:S(2)}) %all-to-all-start.3) | async-done | bytes 10485792 | tf_op jit(solution)/shard_map/all_to_all | solution.py:90
  202.1 13.7 %convolution_convert_fusion.1 = bf16[1024,640]{1,0:T(8,128)(2,1)} fusion(bf16[1024,5120]{1,0:T(8,128)(2,1)} %bitcast.28, bf16[5120,640]{1,0:T(8,128)(2,1)} %all-gather.2.cloned.1.call-done), kind=kOutput, calls=%fused_computation.95 | convolution fusion | flops 6711541760 | bytes 18350080 | tf_op jit(solution)/shard_map/dot_general | solution.py:93
  220.3 182.3 %while.18 = (s32[]{:T(128)}, bf16[5,16,64,128]{3,2,1,0:T(8,128)(2,1)}, bf16[5,16,64,128]{3,2,1,0:T(8,128)(2,1)}, bf16[5,16,64,128]{3,1,2,0:T(8,128)(2,1)}, bf16[...) while((s32[]{:T(128)}, ...), condition=%wide.region_6.8_spmd, body=%wide.region_2.7_spmd.sunk | while | flops 1219638656 | bytes 88276472 | solution.py:106
  225.9 4.0 broadcast_select_fusion.6
  232.5 3.6 fusion.136
  242.5 7.2 %fusion.138 = bf16[5,16,64,128]{3,1,2,0:T(8,128)(2,1)} fusion(bf16[5,16,64,128]{3,1,2,0:T(8,128)(2,1)} %get-tuple-element.341, s32[]{:T(128)S(6)} %copy.142, f32[16,8,64,128]{3,2,1,0:T(8,128)} %bitcast.173, s32[16,8]{0,1:T(8,128)S(1)} %copy.132), kind=kOutput, calls=%fused_computation.26.clone.1 | convolution fusion | flops 201459712 | bytes 4456964 | tf_op jit(solution)/shard_map/while/body/eval_jaxpr/anb,antd->btd/dot_general | solution.py:55
  251.7 5.1 fusion.140
  262.3 4.0 broadcast_select_fusion.6
  278.9 7.3 %fusion.138 = bf16[5,16,64,128]{3,1,2,0:T(8,128)(2,1)} fusion(bf16[5,16,64,128]{3,1,2,0:T(8,128)(2,1)} %get-tuple-element.341, s32[]{:T(128)S(6)} %copy.142, f32[16,8,64,128]{3,2,1,0:T(8,128)} %bitcast.173, s32[16,8]{0,1:T(8,128)S(1)} %copy.132), kind=kOutput, calls=%fused_computation.26.clone.1 | convolution fusion | flops 201459712 | bytes 4456964 | tf_op jit(solution)/shard_map/while/body/eval_jaxpr/anb,antd->btd/dot_general | solution.py:55
  288.1 5.1 fusion.140
  298.7 4.0 broadcast_select_fusion.6
  305.2 3.6 fusion.136
  315.3 7.3 %fusion.138 = bf16[5,16,64,128]{3,1,2,0:T(8,128)(2,1)} fusion(bf16[5,16,64,128]{3,1,2,0:T(8,128)(2,1)} %get-tuple-element.341, s32[]{:T(128)S(6)} %copy.142, f32[16,8,64,128]{3,2,1,0:T(8,128)} %bitcast.173, s32[16,8]{0,1:T(8,128)S(1)} %copy.132), kind=kOutput, calls=%fused_computation.26.clone.1 | convolution fusion | flops 201459712 | bytes 4456964 | tf_op jit(solution)/shard_map/while/body/eval_jaxpr/anb,antd->btd/dot_general | solution.py:55
  324.5 5.1 fusion.140
  335.1 4.0 broadcast_select_fusion.6
  351.7 7.3 %fusion.138 = bf16[5,16,64,128]{3,1,2,0:T(8,128)(2,1)} fusion(bf16[5,16,64,128]{3,1,2,0:T(8,128)(2,1)} %get-tuple-element.341, s32[]{:T(128)S(6)} %copy.142, f32[16,8,64,128]{3,2,1,0:T(8,128)} %bitcast.173, s32[16,8]{0,1:T(8,128)S(1)} %copy.132), kind=kOutput, calls=%fused_computation.26.clone.1 | convolution fusion | flops 201459712 | bytes 4456964 | tf_op jit(solution)/shard_map/while/body/eval_jaxpr/anb,antd->btd/dot_general | solution.py:55
  360.9 5.1 fusion.140
  371.4 4.0 broadcast_select_fusion.6
  388.1 7.3 %fusion.138 = bf16[5,16,64,128]{3,1,2,0:T(8,128)(2,1)} fusion(bf16[5,16,64,128]{3,1,2,0:T(8,128)(2,1)} %get-tuple-element.341, s32[]{:T(128)S(6)} %copy.142, f32[16,8,64,128]{3,2,1,0:T(8,128)} %bitcast.173, s32[16,8]{0,1:T(8,128)S(1)} %copy.132), kind=kOutput, calls=%fused_computation.26.clone.1 | convolution fusion | flops 201459712 | bytes 4456964 | tf_op jit(solution)/shard_map/while/body/eval_jaxpr/anb,antd->btd/dot_general | solution.py:55
  397.3 5.2 fusion.140
  405.0 11.5 %fusion.68 = bf16[5120,640]{0,1:T(8,128)(2,1)} fusion(bf16[1024,5120]{1,0:T(8,128)(2,1)} %bitcast.28, bf16[128,8,5,128]{3,2,1,0:T(8,128)(2,1)S(1)} %bitcast.193), kind=kOutput, calls=%fused_computation.66 | convolution fusion | flops 6717440000 | bytes 18350080 | tf_op jit(solution)/shard_map/td,te->de/dot_general | solution.py:116
  416.6 9.5 %copy.97 = bf16[5120,640]{1,0:T(8,128)(2,1)} copy(bf16[5120,640]{0,1:T(8,128)(2,1)} %fusion.68) | data formatting | bytes 13107200
  443.9 4.3 all-to-all-done.4
  449.3 3.8 all-to-all-start.5
  467.6 4.8 all-to-all-start.6
  487.7 25.8 %reduce-scatter.4.cloned.1.call-done = bf16[160,640]{1,0:T(8,128)(2,1)} async-done(((bf16[5120,640]{1,0:T(8,128)(2,1)}), bf16[160,640]{1,0:T(8,128)(2,1)}) %reduce-scatter.4.cloned.1.call-update) | async-done | bytes 204816
  (229 shorter events, 180.4 us)
Async XLA Ops:
  7.2 82.1 %copy-start = (s32[1,16]{1,0:T(1,128)S(1)}, s32[1,16]{1,0:T(1,128)}, u32[]{:S(2)}) copy-start(s32[1,16]{1,0:T(1,128)} %param.19) | copy-start | bytes 196
  7.2 194.9 %all-gather.2.cloned.1.call-start = ((), (), s32[]{:S(2)}) async-start(), calls=%async_computation.8 | async-start | bytes 6758400 | tf_op jit(solution)/shard_map/all_gather | solution.py:94
  12.5 22.5 %all-to-all-start = ((bf16[256,4,640]{2,0,1:T(8,128)(2,1)}), bf16[256,4,640]{2,0,1:T(8,128)(2,1)S(1)}, u32[]{:S(2)}, u32[]{:S(2)}) async-start(bf16[256,4,640]{2,0,1:T(8,128)(2,1)} %copy.73), calls=%async_computation | async-start | bytes 2621440 | tf_op jit(solution)/shard_map/all_to_all | solution.py:84
  18.7 4.9 copy-start.5
  19.6 3.9 copy-start.20
  34.9 20.5 %all-to-all-start.1 = ((bf16[256,4,640]{2,0,1:T(8,128)(2,1)}), bf16[256,4,640]{2,0,1:T(8,128)(2,1)S(1)}, u32[]{:S(2)}, u32[]{:S(2)}) async-start(bf16[256,4,640]{2,0,1:T(8,128)(2,1)} %copy.75), calls=%async_computation.1 | async-start | bytes 2621440 | tf_op jit(solution)/shard_map/all_to_all | solution.py:85
  55.5 27.3 %copy-start.11 = (bf16[256,4,640]{2,0,1:T(8,128)(2,1)}, bf16[256,4,640]{2,0,1:T(8,128)(2,1)S(1)}, u32[]{:S(2)}) copy-start(bf16[256,4,640]{2,0,1:T(8,128)(2,1)S(1)} %all-to-all-done.1) | copy-start | bytes 3932164
  82.8 6.2 %copy-start.19 = (s32[16,8]{0,1:T(8,128)S(1)}, s32[16,8]{0,1:T(8,128)}, u32[]{:S(2)}) copy-start(s32[16,8]{0,1:T(8,128)} %param.18) | copy-start | bytes 1540
  82.8 119.3 %all-to-all-start.3 = ((bf16[4,256,5120]{2,1,0:T(8,128)(2,1)}), bf16[4,256,5120]{2,1,0:T(8,128)(2,1)}, u32[]{:S(2)}, u32[]{:S(2)}) async-start(bf16[4,256,5120]{2,1,0:T(8,128)(2,1)} %stack.2), calls=%async_computation.3 | async-start | bytes 20971520 | tf_op jit(solution)/shard_map/all_to_all | solution.py:90
  88.9 424.6 %reduce-scatter.4.cloned.1.call-start = ((), (), s32[]{:S(2)}) async-start(), calls=%async_computation.9 | async-start | bytes 6758400
  232.5 3.6 copy-start.2
  232.5 3.6 copy-start.3
  242.5 7.3 %copy-start.4 = (f32[16,64,512]{2,1,0:T(8,128)S(1)}, f32[16,64,512]{2,1,0:T(8,128)}, u32[]{:S(2)}) copy-start(f32[16,64,512]{2,1,0:T(8,128)} %get-tuple-element.322) | copy-start | bytes 6291460 | tf_op jit(solution)/shard_map/while
  268.9 3.6 copy-start.2
  268.9 3.6 copy-start.3
  278.9 7.3 %copy-start.4 = (f32[16,64,512]{2,1,0:T(8,128)S(1)}, f32[16,64,512]{2,1,0:T(8,128)}, u32[]{:S(2)}) copy-start(f32[16,64,512]{2,1,0:T(8,128)} %get-tuple-element.322) | copy-start | bytes 6291460 | tf_op jit(solution)/shard_map/while
  305.2 3.6 copy-start.2
  305.2 3.6 copy-start.3
  315.3 7.3 %copy-start.4 = (f32[16,64,512]{2,1,0:T(8,128)S(1)}, f32[16,64,512]{2,1,0:T(8,128)}, u32[]{:S(2)}) copy-start(f32[16,64,512]{2,1,0:T(8,128)} %get-tuple-element.322) | copy-start | bytes 6291460 | tf_op jit(solution)/shard_map/while
  341.6 3.6 copy-start.2
  341.6 3.6 copy-start.3
  351.7 7.3 %copy-start.4 = (f32[16,64,512]{2,1,0:T(8,128)S(1)}, f32[16,64,512]{2,1,0:T(8,128)}, u32[]{:S(2)}) copy-start(f32[16,64,512]{2,1,0:T(8,128)} %get-tuple-element.322) | copy-start | bytes 6291460 | tf_op jit(solution)/shard_map/while
  378.0 3.6 copy-start.2
  378.0 3.6 copy-start.3
  388.1 7.3 %copy-start.4 = (f32[16,64,512]{2,1,0:T(8,128)S(1)}, f32[16,64,512]{2,1,0:T(8,128)}, u32[]{:S(2)}) copy-start(f32[16,64,512]{2,1,0:T(8,128)} %get-tuple-element.322) | copy-start | bytes 6291460 | tf_op jit(solution)/shard_map/while
  430.8 17.4 %all-to-all-start.4 = ((bf16[4,256,640]{2,1,0:T(8,128)(2,1)}), bf16[4,256,640]{2,1,0:T(8,128)(2,1)S(1)}, u32[]{:S(2)}, u32[]{:S(2)}) async-start(bf16[4,256,640]{2,1,0:T(8,128)(2,1)} %all_to_all.83), calls=%async_computation.4 | async-start | bytes 2621440 | tf_op jit(solution)/shard_map/all_to_all | solution.py:124
  449.3 17.3 %all-to-all-start.5 = ((bf16[4,256,640]{2,1,0:T(8,128)(2,1)}), bf16[4,256,640]{2,1,0:T(8,128)(2,1)S(1)}, u32[]{:S(2)}, u32[]{:S(2)}) async-start(bf16[4,256,640]{2,1,0:T(8,128)(2,1)} %all_to_all.85), calls=%async_computation.5 | async-start | bytes 2621440 | tf_op jit(solution)/shard_map/all_to_all | solution.py:125
  456.2 3.4 copy-start.16
  467.6 17.9 %all-to-all-start.6 = ((bf16[4,256,640]{2,1,0:T(8,128)(2,1)}), bf16[4,256,640]{2,1,0:T(8,128)(2,1)S(1)}, u32[]{:S(2)}, u32[]{:S(2)}) async-start(bf16[4,256,640]{2,1,0:T(8,128)(2,1)} %all_to_all.87), calls=%async_computation.6 | async-start | bytes 2621440 | tf_op jit(solution)/shard_map/all_to_all | solution.py:126
  475.3 3.4 copy-start.6
  475.3 3.4 copy-start.18
  485.5 30.0 %copy-start.1 = (s32[1,16]{1,0:T(1,128)S(1)}, s32[1,16]{1,0:T(1,128)}, u32[]{:S(2)}) copy-start(s32[1,16]{1,0:T(1,128)} %param.19) | copy-start | bytes 196
  (14 other events, 32.2 us)
Sparse Core Ops, SparseCore 0:
  10.3 52.1 all-gather.1
  426.2 87.2 reduce-scatter.3
